TPU v7x, 32 devices: a whole 2x2x4 slice. The times are simulated.
32 devices in a mesh: band: 4 (over y, x), sector: 8 (over z, core).
Axes of the slice: x: 2, y: 2, z: 4, core: 2. Of those that a mesh axis runs over, the one named last changes fastest.
Arguments:
- grid_lat: bfloat16 [32, 512, 512], P('band', 'sector'), may hold values from -6 to 6
- mesh_lat: bfloat16 [4096, 512], P(('band', 'sector')), may hold values from -6 to 6
- edge_feat: bfloat16 [49152, 512], P(('band', 'sector')), may hold values from -6 to 6
- edge_src: int32 [49152], P(('band', 'sector')), may hold values from 0 to 255, as said below
- edge_dst: int32 [49152], P(('band', 'sector')), may hold values from 0 to 511, as said below
- send_rows: int32 [4096], P(('band', 'sector')), may hold values from 0 to 127
- w_edge1: bfloat16 [1536, 512], replicated, may hold values from -0.15625 to 0.15625
- w_edge2: bfloat16 [512, 512], replicated, may hold values from -0.25 to 0.25
- edge_gain: float32 [512], replicated, may hold values from 0.25 to 1.75
- w_node1: bfloat16 [1024, 512], replicated, may hold values from -0.1875 to 0.1875
- w_node2: bfloat16 [512, 512], replicated, may hold values from -0.25 to 0.25
- node_gain: float32 [512], replicated, may hold values from 0.25 to 1.75
- cotangent: bfloat16 [32, 512, 512], P('band', 'sector'), may hold values from -6 to 6
Outputs:
- grid_out: bfloat16 [32, 512, 512], P('band', 'sector')
- grad_grid: bfloat16 [32, 512, 512], P('band', 'sector')
- grad_mesh: bfloat16 [4096, 512], P(('band', 'sector'))
- grad_w_edge1: float32 [1536, 512], P('sector')
Inputs may be any that keep to these rules, and one draw needn't show every extreme that they name: `edge_src`: A device's mesh table is its 128 own rows followed by 32 rows each from the sector neighbour below, the sector neighbour above, the band neighbour below and the band neighbour above; devices of the first band never read the rows from below, those of the last band never the rows from above. `edge_dst`: each grid point of a device is the destination of exactly 3 of that device's edges; edges are in no particular order.
All inputs are finite; a program needn't handle non-finite values.
Results may differ from a plain program's by a relative error of at most 0.02.
Values may be sent and summed in bfloat16 or wider, within the bound.
A program may use at most 64 MiB of HBM per device.

v0:
```python
import math

import jax
import jax.numpy as jnp
from jax import lax
from jax.sharding import PartitionSpec as P

EPSILON = 1e-05


def with_halo(shard, sides, width, wrap):
    for axis, dim in sides:
        devices, length = (lax.axis_size(axis), shard.shape[dim])
        up = [(i, (i + 1) % devices) for i in range(devices if wrap else devices - 1)]
        down = [(j, i) for i, j in up]
        last = lax.slice_in_dim(shard, length - width, length, axis=dim)
        initial = lax.slice_in_dim(shard, 0, width, axis=dim)
        before = lax.ppermute(last, axis, up)
        after = lax.ppermute(initial, axis, down)
        shard = jnp.concatenate([before, shard, after], axis=dim)
    return shard


def swish(values):
    return values * jax.nn.sigmoid(values)


def layer_norm(values, gain_vector):
    average = jnp.mean(values, axis=-1, keepdims=True)
    centred = values - average
    spread = jnp.mean(centred * centred, axis=-1, keepdims=True)
    return centred * lax.rsqrt(spread + EPSILON) * gain_vector


def decode_tail(pre_act, grid_wide, edge_dst, w_edge2, edge_gain, w_node1, w_node2, node_gain):
    hidden = swish(pre_act).astype(jnp.bfloat16)
    edge_raw = jnp.dot(hidden, w_edge2, preferred_element_type=jnp.float32)
    message = layer_norm(edge_raw, edge_gain).astype(jnp.bfloat16)
    points = grid_wide.shape[0]
    onehot = (edge_dst[None, :] == jnp.arange(points, dtype=jnp.int32)[:, None]).astype(
        jnp.bfloat16
    )
    aggregated = jnp.dot(onehot, message, preferred_element_type=jnp.float32).astype(jnp.bfloat16)
    node_input = jnp.concatenate([aggregated, grid_wide.astype(jnp.bfloat16)], axis=1)
    node_hidden = swish(jnp.dot(node_input, w_node1, preferred_element_type=jnp.float32)).astype(
        jnp.bfloat16
    )
    node_raw = jnp.dot(node_hidden, w_node2, preferred_element_type=jnp.float32)
    return (grid_wide + layer_norm(node_raw, node_gain)).astype(jnp.bfloat16)


def shards(
    grid_lat,
    mesh_lat,
    edge_feat,
    edge_src,
    edge_dst,
    send_rows,
    w_edge1,
    w_edge2,
    edge_gain,
    w_node1,
    w_node2,
    node_gain,
    cotangent,
):
    feature_width = w_edge2.shape[0]
    lat_rows = grid_lat.shape[0]
    lon_cols = grid_lat.shape[1]
    grid_block = grid_lat.reshape(lat_rows * lon_cols, feature_width)
    cot_block = cotangent.reshape(lat_rows * lon_cols, feature_width)
    own_rows = mesh_lat.shape[0]
    margin = send_rows.shape[0] // 4
    picked = jnp.take(mesh_lat, send_rows, axis=0)
    sector_recv = with_halo(picked[: 2 * margin], (("sector", 0),), margin, True)
    band_recv = with_halo(picked[2 * margin :], (("band", 0),), margin, False)
    mesh_table = jnp.concatenate(
        [
            mesh_lat,
            sector_recv[:margin],
            sector_recv[3 * margin :],
            band_recv[:margin],
            band_recv[3 * margin :],
        ],
        axis=0,
    )
    inputs = jnp.concatenate([edge_feat, mesh_table[edge_src], grid_block[edge_dst]], axis=1)
    pre_act = jnp.dot(inputs, w_edge1, preferred_element_type=jnp.float32)
    grid_wide = grid_block.astype(jnp.float32)

    def finish(pre_values, grid_values):
        return decode_tail(
            pre_values, grid_values, edge_dst, w_edge2, edge_gain, w_node1, w_node2, node_gain
        )

    result, pullback = jax.vjp(finish, pre_act, grid_wide)
    grad_pre, grad_tail = pullback(cot_block)
    grad_pre_b = grad_pre.astype(jnp.bfloat16)
    grad_inputs = lax.dot_general(
        grad_pre_b,
        w_edge1[feature_width:],
        (((1,), (1,)), ((), ())),
        preferred_element_type=jnp.float32,
    )
    grad_table = jax.ops.segment_sum(
        grad_inputs[:, :feature_width], edge_src, num_segments=mesh_table.shape[0]
    )
    grad_grid = grad_tail + jax.ops.segment_sum(
        grad_inputs[:, feature_width:], edge_dst, num_segments=grid_block.shape[0]
    )
    sector_back = with_halo(
        grad_table[own_rows : own_rows + 2 * margin].astype(jnp.bfloat16),
        (("sector", 0),),
        margin,
        True,
    ).astype(jnp.float32)
    band_back = with_halo(
        grad_table[own_rows + 2 * margin :].astype(jnp.bfloat16), (("band", 0),), margin, False
    ).astype(jnp.float32)
    returned = jnp.concatenate(
        [
            sector_back[:margin],
            sector_back[3 * margin :],
            band_back[:margin],
            band_back[3 * margin :],
        ],
        axis=0,
    )
    grad_mesh = (
        grad_table[:own_rows] + jax.ops.segment_sum(returned, send_rows, num_segments=own_rows)
    ).astype(jnp.bfloat16)
    total_edges = edge_feat.shape[0] * lax.axis_size("band") * lax.axis_size("sector")
    grad_scale = 1.0 / math.sqrt(total_edges)
    sector_part = lax.psum_scatter(
        lax.dot_general(
            inputs, grad_pre_b, (((0,), (0,)), ((), ())), preferred_element_type=jnp.float32
        ).astype(jnp.bfloat16),
        "sector",
        scatter_dimension=0,
        tiled=True,
    )
    share_rows = lax.psum(sector_part, "band").astype(jnp.float32)
    grad_w_edge1 = share_rows * grad_scale
    grid_out = result.reshape(lat_rows, lon_cols, feature_width)
    grad_grid_out = grad_grid.astype(jnp.bfloat16).reshape(lat_rows, lon_cols, feature_width)
    return (grid_out, grad_grid_out, grad_mesh, grad_w_edge1)


def solution(mesh):
    in_specs = (
        P("band", "sector", None),
        P(("band", "sector"), None),
        P(("band", "sector"), None),
        P(("band", "sector")),
        P(("band", "sector")),
        P(("band", "sector")),
        P(),
        P(),
        P(),
        P(),
        P(),
        P(),
        P("band", "sector", None),
    )
    out_specs = (
        P("band", "sector", None),
        P("band", "sector", None),
        P(("band", "sector"), None),
        P("sector", None),
    )
    return jax.shard_map(shards, mesh=mesh, in_specs=in_specs, out_specs=out_specs, check_vma=False)
```

profile of v0, /device:TPU:0, one launch (start us, length us, event | category | flops | bytes accessed | tf_op | source)
XLA Modules:
  0.0 159.2 jit_solution(11389695265624207588)
XLA Ops:
  7.2 0.0 copy-start
  7.2 0.0 reduce-scatter.2.cloned.1.call-start
  7.2 0.8 compare_and_fusion
  8.0 0.7 compare_select_fusion.2
  8.7 1.8 %gather_fusion = bf16[128,512]{1,0:T(8,128)(2,1)S(1)} fusion(bf16[128,512]{1,0:T(8,128)(2,1)} %param.14, s32[1024]{0:T(1024)S(1)} %pad_clamp_fusion.2), kind=kCustom, calls=%fused_computation | custom fusion | bytes 262656 | tf_op jit(solution)/shard_map/jit(_take)/gather | solution.py:74
  10.5 0.1 broadcast_select_fusion
  10.6 0.7 fusion.66
  11.2 1.3 collective-permute-start.3
  12.5 5.5 %collective-permute-start.2 = (bf16[32,512]{1,0:T(8,128)(2,1)}, bf16[32,512]{1,0:T(8,128)(2,1)S(1)}, u32[]{:S(2)}, u32[]{:S(2)}) collective-permute-start(bf16[32,512]{1,0:T(8,128)(2,1)} %get-tuple-element.20), channel_id=1, source_target_pairs={{0,8},{8,16},{16,24},{1,9},{9,17},{17,25},{2,10},{10,18},{18,26},{... | collective-permute-start | bytes 98312 | tf_op jit(solution)/shard_map/ppermute | solution.py:18
  18.0 3.1 %collective-permute-start.1 = (bf16[32,512]{1,0:T(8,128)(2,1)}, bf16[32,512]{1,0:T(8,128)(2,1)S(1)}, u32[]{:S(2)}, u32[]{:S(2)}) collective-permute-start(bf16[32,512]{1,0:T(8,128)(2,1)} %get-tuple-element.21), channel_id=1, source_target_pairs={{1,0},{2,1},{3,2},{4,3},{5,4},{6,5},{7,6},{0,7},{9,8},{10,9},{11,1... | collective-permute-start | bytes 98312 | tf_op jit(solution)/shard_map/ppermute | solution.py:19
  21.1 0.0 collective-permute-start
  21.1 0.9 constant_dynamic-update-slice_fusion.4
  22.0 0.7 compare_select_fusion.1
  22.7 0.7 compare_select_fusion
  23.4 2.7 %constant_dynamic-update-slice_fusion.7 = bf16[1536,1536]{1,0:T(8,128)(2,1)} fusion(bf16[1536,512]{1,0:T(8,128)(2,1)} %param.15), kind=kLoop, calls=%fused_computation.96 | loop fusion | bytes 3145728
  26.1 4.8 %gather_fusion.2 = bf16[1536,512]{1,0:T(8,128)(2,1)S(1)} fusion(bf16[512,512]{1,0:T(8,128)(2,1)S(1)} %bitcast.21, s32[2048]{0:T(1024)S(1)} %pad_clamp_fusion), kind=kCustom, calls=%fused_computation.2 | custom fusion | bytes 3151872 | tf_op jit(solution)/shard_map/gather | solution.py:87
  31.0 0.0 collective-permute-done.1
  31.0 0.0 collective-permute-done.2
  31.0 0.0 collective-permute-done.3
  31.0 5.4 %gather_fusion.1 = bf16[1536,512]{1,0:T(8,128)(2,1)} fusion(bf16[256,512]{1,0:T(8,128)(2,1)S(1)} %constant_dynamic-update-slice_fusion, s32[2048]{0:T(1024)S(1)} %pad_clamp_fusion.1), kind=kCustom, calls=%fused_computation.1 | custom fusion | bytes 3151872 | tf_op jit(solution)/shard_map/gather | solution.py:87
  36.5 2.8 %constant_dynamic-update-slice_fusion.6 = bf16[1536,1536]{1,0:T(8,128)(2,1)} fusion(bf16[1536,1536]{1,0:T(8,128)(2,1)} %constant_dynamic-update-slice_fusion.7, bf16[1536,512]{1,0:T(8,128)(2,1)} %gather_fusion.1), kind=kLoop, calls=%fused_computation.95 | loop fusion | bytes 3145728
  39.3 1.3 constant_dynamic-update-slice_fusion.5
  40.6 4.5 %fusion.69 = f32[1536,512]{1,0:T(8,128)S(1)} fusion(bf16[1536,1536]{1,0:T(8,128)(2,1)} %constant_dynamic-update-slice_fusion.5, bf16[1536,512]{1,0:T(8,128)(2,1)S(1)} %copy-done.8), kind=kOutput, calls=%fused_computation.122 | convolution fusion | flops 2415919104 | bytes 9437184 | tf_op jit(solution)/shard_map/dot_general | solution.py:88
  45.1 1.2 fusion.67
  46.3 0.5 copy-done.14
  46.8 0.4 multiply_reduce_fusion.1
  47.2 0.3 copy-done.6
  47.4 0.0 copy-done.7
  47.5 1.2 fusion.24
  48.7 0.0 copy-start.9
  48.7 0.7 fusion.32
  49.4 0.3 copy-done.9
  49.7 0.5 fusion.68
  50.3 0.5 copy-done.13
  50.7 0.4 copy-done.4
  51.1 0.4 fusion.27
  51.6 1.3 fusion.63
  52.9 3.6 %convolution_convert_fusion.1 = bf16[512,1024]{1,0:T(8,128)(2,1)} fusion(bf16[1024,512]{1,0:T(8,128)(2,1)S(1)} %copy-done, f32[512,512]{1,0:T(8,128)} %copy-done.13, bf16[512,512]{1,0:T(8,128)(2,1)} %param.23, f32[512,512]{1,0:T(8,128)S(1)} %get-tuple-element.7, f32[512]{0:T(512)S(1)} %negate_multiply_fusion.1), kind=kOutput, calls=%fused_computation.40 | convolution fusion | flops 808976384 | bytes 4720640 | tf_op jit(solution)/shard_map/transpose(jvp())/dot_general | solution.py:45
  56.5 3.5 %multiply_reduce_fusion = (f32[1536]{0:T(1024)S(1)}, bf16[1536,512]{0,1:T(8,128)(2,1)S(1)}) fusion(f32[1536,512]{0,1:T(8,128)} %copy-done.2, f32[512]{0:T(512)S(1)} %copy-done.7, f32[1536]{0:T(1024)S(1)} %broadcast_multiply_fusion, bf16[512,1024]{1,0:T(8,128)(2,1)} %convolution_convert_fusion.1, s32[1536]{0:T(1024)S(1)} %copy-done.6), kind=kOutput, calls=%fused_computation.19 | convolution fusion | flops 810809856 | bytes 5263360 | tf_op jit(solution)/shard_map/transpose(jvp())/dot_general | solution.py:43
  60.0 0.0 copy-start.11
  60.0 0.0 slice-start
  60.0 0.9 fusion.45
  60.9 0.1 copy-done.11
  61.0 1.0 copy-done.15
  62.0 2.4 %fusion.1 = bf16[1536,512]{1,0:T(8,128)(2,1)S(1)} fusion(f32[1536,512]{1,0:T(8,128)S(1)} %copy-done.15, bf16[512,512]{1,0:T(8,128)(2,1)S(1)} %copy-done.11, f32[1536]{0:T(1024)S(1)} %negate_multiply_fusion, bf16[1536,512]{0,1:T(8,128)(2,1)S(1)} %get-tuple-element.30, f32[1536,512]{0,1:T(8,128)S(1)} %copy-done.3, f32[1536]{0:T(1024)S(1)} %multiply_multiply_fusion, ...), kind=kOutput, calls=%fused_computation.11 | convolution fusion | flops 821035008 | bytes 9988096 | tf_op jit(solution)/shard_map/transpose(jvp())/dot_general | solution.py:37
  64.5 1.2 copy-done.12
  65.7 3.8 %convolution_convert_fusion = bf16[1536,512]{1,0:T(8,128)(2,1)} fusion(bf16[1536,1536]{1,0:T(8,128)(2,1)S(1)} %bitcast.26, bf16[1536,512]{1,0:T(8,128)(2,1)S(1)} %fusion.1), kind=kOutput, calls=%fused_computation.30 | convolution fusion | flops 2416705536 | bytes 7864320 | tf_op jit(solution)/shard_map/dot_general | solution.py:135
  69.5 0.0 reduce-scatter.2.cloned.1.call-update
  69.5 0.0 all-reduce.2.cloned.1.call-start
  69.5 6.2 %fusion.36 = f32[1536,1024]{1,0:T(8,128)} fusion(bf16[1536,512]{1,0:T(8,128)(2,1)} %copy-done.12, bf16[1536,512]{1,0:T(8,128)(2,1)} %param.19), kind=kOutput, calls=%fused_computation.56 | convolution fusion | flops 1610612736 | bytes 8912896 | tf_op jit(solution)/shard_map/dot_general | solution.py:99
  75.7 10.7 %scatter_custom_fusion.1 = f32[256,512]{1,0:T(8,128)S(1)} fusion(s32[1536]{0:T(1024)} %param.16, f32[1536,1024]{1,0:T(8,128)} %fusion.36, f32[]{:T(128)} %constant.21.clone.1), kind=kCustom, calls=%fused_computation.13 | custom fusion | flops 786432 | bytes 3670528 | tf_op jit(solution)/shard_map/scatter-add | solution.py:105
  86.5 1.3 collective-permute-start.7
  87.8 4.9 %collective-permute-start.6 = (bf16[32,512]{1,0:T(8,128)(2,1)S(1)}, bf16[32,512]{1,0:T(8,128)(2,1)S(1)}, u32[]{:S(2)}, u32[]{:S(2)}) collective-permute-start(bf16[32,512]{1,0:T(8,128)(2,1)S(1)} %get-tuple-element.11), channel_id=1, source_target_pairs={{0,8},{8,16},{16,24},{1,9},{9,17},{17,25},{2,10},{10,18},{18,26},{... | collective-permute-start | bytes 98312 | tf_op jit(solution)/shard_map/ppermute | solution.py:18
  92.6 1.2 convert_add_fusion
  93.9 10.9 %scatter_custom_fusion = f32[512,512]{1,0:T(8,128)S(1)} fusion(f32[512,512]{1,0:T(8,128)S(1)} %convert_add_fusion, s32[1536]{0:T(1024)S(1)} %copy-done.6, f32[1536,1024]{1,0:T(8,128)} %fusion.36), kind=kCustom, calls=%fused_computation.15 | custom fusion | flops 786432 | bytes 4194304 | tf_op jit(solution)/shard_map/scatter-add | solution.py:108
  104.7 0.9 convert_element_type.91
  105.6 3.5 %collective-permute-start.5 = (bf16[32,512]{1,0:T(8,128)(2,1)S(1)}, bf16[32,512]{1,0:T(8,128)(2,1)S(1)}, u32[]{:S(2)}, u32[]{:S(2)}) collective-permute-start(bf16[32,512]{1,0:T(8,128)(2,1)S(1)} %get-tuple-element.12), channel_id=1, source_target_pairs={{1,0},{2,1},{3,2},{4,3},{5,4},{6,5},{7,6},{0,7},{9,8},{10,9},{11,1... | collective-permute-start | bytes 98312 | tf_op jit(solution)/shard_map/ppermute | solution.py:19
  109.1 0.0 all-reduce.2.cloned.1.call-update
  109.2 1.5 collective-permute-done.4
  110.7 0.0 collective-permute-done.5
  110.8 1.6 %scatter_custom_fusion.2 = f32[128,512]{1,0:T(8,128)S(1)} fusion(f32[128,512]{1,0:T(8,128)S(1)} %slice.96, s32[128]{0:T(128)} %param.18, f32[32,512]{1,0:T(8,128)S(1)} %get-tuple-element.18, f32[]{:T(128)} %constant.48, f32[32,512]{1,0:T(8,128)S(1)} %get-tuple-element.17, f32[32,512]{1,0:T(8,128)S(1)} %get-tuple-element.16, f32[32,512]{1,0:T(8,128)S(1)} %get-tuple-element.15), kind=kCustom, calls=%fused_computation.69 | custom fusion | flops 262144 | bytes 524800 | tf_op jit(solution)/shard_map/scatter-add | solution.py:130
  112.4 0.7 convert_element_type.94
  113.1 37.5 %all-reduce.2.cloned.1.call-done = bf16[192,512]{1,0:T(8,128)(2,1)} async-done(((bf16[192,512]{1,0:T(8,128)(2,1)}), bf16[192,512]{1,0:T(8,128)(2,1)}) %all-reduce.2.cloned.1.call-update) | async-done | bytes 196624 | tf_op jit(solution)/shard_map/psum | solution.py:142
  150.6 1.7 %convert_multiply_fusion.6 = f32[192,512]{1,0:T(8,128)} fusion(bf16[192,512]{1,0:T(8,128)(2,1)} %all-reduce.2.cloned.1.call-done), kind=kLoop, calls=%fused_computation.68 | loop fusion | flops 196608 | bytes 589824 | tf_op jit(solution)/shard_map/mul | solution.py:143
  (49 shorter events, 0.3 us)
Async XLA Ops:
  7.2 41.5 %copy-start = (bf16[1024,512]{1,0:T(8,128)(2,1)S(1)}, bf16[1024,512]{1,0:T(8,128)(2,1)}, u32[]{:S(2)}) copy-start(bf16[1024,512]{1,0:T(8,128)(2,1)} %param.22) | copy-start | bytes 3145732
  7.2 19.0 %copy-start.1 = (bf16[8,64,512]{2,1,0:T(8,128)(2,1)S(1)}, bf16[8,64,512]{2,1,0:T(8,128)(2,1)}, u32[]{:S(2)}) copy-start(bf16[8,64,512]{2,1,0:T(8,128)(2,1)} %param.13) | copy-start | bytes 1572868
  7.2 102.0 %reduce-scatter.2.cloned.1.call-start = ((), (), s32[]{:S(2)}) async-start(), calls=%async_computation.1 | async-start | bytes 1769472 | tf_op jit(solution)/shard_map/reduce_scatter | solution.py:134
  11.2 19.8 %collective-permute-start.3 = (bf16[32,512]{1,0:T(8,128)(2,1)}, bf16[32,512]{1,0:T(8,128)(2,1)S(1)}, u32[]{:S(2)}, u32[]{:S(2)}) collective-permute-start(bf16[32,512]{1,0:T(8,128)(2,1)} %get-tuple-element.19), channel_id=1, source_target_pairs={{8,0},{16,8},{24,16},{9,1},{17,9},{25,17},{10,2},{18,10},{26,18},{... | collective-permute-start | bytes 98312 | tf_op jit(solution)/shard_map/ppermute | solution.py:19
  12.5 18.5 %collective-permute-start.2 = (bf16[32,512]{1,0:T(8,128)(2,1)}, bf16[32,512]{1,0:T(8,128)(2,1)S(1)}, u32[]{:S(2)}, u32[]{:S(2)}) collective-permute-start(bf16[32,512]{1,0:T(8,128)(2,1)} %get-tuple-element.20), channel_id=1, source_target_pairs={{0,8},{8,16},{16,24},{1,9},{9,17},{17,25},{2,10},{10,18},{18,26},{... | collective-permute-start | bytes 98312 | tf_op jit(solution)/shard_map/ppermute | solution.py:18
  18.0 13.0 %collective-permute-start.1 = (bf16[32,512]{1,0:T(8,128)(2,1)}, bf16[32,512]{1,0:T(8,128)(2,1)S(1)}, u32[]{:S(2)}, u32[]{:S(2)}) collective-permute-start(bf16[32,512]{1,0:T(8,128)(2,1)} %get-tuple-element.21), channel_id=1, source_target_pairs={{1,0},{2,1},{3,2},{4,3},{5,4},{6,5},{7,6},{0,7},{9,8},{10,9},{11,1... | collective-permute-start | bytes 98312 | tf_op jit(solution)/shard_map/ppermute | solution.py:19
  21.1 9.9 %collective-permute-start = (bf16[32,512]{1,0:T(8,128)(2,1)}, bf16[32,512]{1,0:T(8,128)(2,1)S(1)}, u32[]{:S(2)}, u32[]{:S(2)}) collective-permute-start(bf16[32,512]{1,0:T(8,128)(2,1)} %get-tuple-element.22), channel_id=1, source_target_pairs={{0,1},{1,2},{2,3},{3,4},{4,5},{5,6},{6,7},{7,0},{8,9},{9,10},{10,1... | collective-permute-start | bytes 98312 | tf_op jit(solution)/shard_map/ppermute | solution.py:18
  36.5 4.1 %copy-start.8 = (bf16[1536,512]{1,0:T(8,128)(2,1)S(1)}, bf16[1536,512]{1,0:T(8,128)(2,1)}, u32[]{:S(2)}) copy-start(bf16[1536,512]{1,0:T(8,128)(2,1)} %param.19) | copy-start | bytes 4718596
  40.6 4.5 %copy-start.10 = (bf16[512,512]{1,0:T(8,128)(2,1)S(1)}, bf16[512,512]{1,0:T(8,128)(2,1)}, u32[]{:S(2)}) copy-start(bf16[512,512]{1,0:T(8,128)(2,1)} %param.20) | copy-start | bytes 1572868
  45.1 1.6 %copy-start.14 = (f32[1536,512]{1,0:T(8,128)}, f32[1536,512]{1,0:T(8,128)S(1)}, u32[]{:S(2)}) copy-start(f32[1536,512]{1,0:T(8,128)S(1)} %fusion.69) | copy-start | bytes 9437188
  46.8 1.9 %copy-start.2 = (f32[1536,512]{0,1:T(8,128)}, f32[1536,512]{0,1:T(8,128)S(1)}, u32[]{:S(2)}) copy-start(f32[1536,512]{0,1:T(8,128)S(1)} %get-tuple-element.26) | copy-start | bytes 9437188
  46.8 0.7 copy-start.6
  46.8 0.7 copy-start.7
  48.7 1.0 copy-start.9
  49.7 1.0 copy-start.13
  49.7 1.4 copy-start.4
  49.7 1.4 copy-start.5
  56.5 3.5 %copy-start.3 = (f32[1536,512]{0,1:T(8,128)S(1)}, f32[1536,512]{0,1:T(8,128)}, u32[]{:S(2)}) copy-start(f32[1536,512]{0,1:T(8,128)} %copy-done.2) | copy-start | bytes 9437188
  60.0 1.0 copy-start.11
  60.0 2.1 %copy-start.15 = (f32[1536,512]{1,0:T(8,128)S(1)}, f32[1536,512]{1,0:T(8,128)}, u32[]{:S(2)}) copy-start(f32[1536,512]{1,0:T(8,128)} %copy-done.14) | copy-start | bytes 9437188
  60.0 5.7 %slice-start = ((s8[4718592]{0:T(1024)(128)(4,1)}), s8[4194304]{0:T(1024)(128)(4,1)S(1)}, s32[]{:S(2)}) async-start(s8[4718592]{0:T(1024)(128)(4,1)} %bitcast.25), calls=%async_computation.3 | async-start | bytes 8388608
  62.0 3.7 %slice-start.1 = ((s8[4718592]{0:T(1024)(128)(4,1)}), s8[524288]{0:T(1024)(128)(4,1)S(1)}, s32[]{:S(2)}) async-start(s8[4718592]{0:T(1024)(128)(4,1)} %bitcast.25), calls=%async_computation.4 | async-start | bytes 1048576
  64.5 1.2 copy-start.12
  69.5 81.1 %all-reduce.2.cloned.1.call-start = ((), (), s32[]{:S(2)}) async-start(), calls=%async_computation.2 | async-start | bytes 393216 | tf_op jit(solution)/shard_map/psum | solution.py:142
  86.5 22.7 %collective-permute-start.7 = (bf16[32,512]{1,0:T(8,128)(2,1)S(1)}, bf16[32,512]{1,0:T(8,128)(2,1)S(1)}, u32[]{:S(2)}, u32[]{:S(2)}) collective-permute-start(bf16[32,512]{1,0:T(8,128)(2,1)S(1)} %get-tuple-element.10), channel_id=1, source_target_pairs={{8,0},{16,8},{24,16},{9,1},{17,9},{25,17},{10,2},{18,10},{26,18},{... | collective-permute-start | bytes 98312 | tf_op jit(solution)/shard_map/ppermute | solution.py:19
  87.8 21.4 %collective-permute-start.6 = (bf16[32,512]{1,0:T(8,128)(2,1)S(1)}, bf16[32,512]{1,0:T(8,128)(2,1)S(1)}, u32[]{:S(2)}, u32[]{:S(2)}) collective-permute-start(bf16[32,512]{1,0:T(8,128)(2,1)S(1)} %get-tuple-element.11), channel_id=1, source_target_pairs={{0,8},{8,16},{16,24},{1,9},{9,17},{17,25},{2,10},{10,18},{18,26},{... | collective-permute-start | bytes 98312 | tf_op jit(solution)/shard_map/ppermute | solution.py:18
  105.6 5.1 %collective-permute-start.4 = (bf16[32,512]{1,0:T(8,128)(2,1)S(1)}, bf16[32,512]{1,0:T(8,128)(2,1)S(1)}, u32[]{:S(2)}, u32[]{:S(2)}) collective-permute-start(bf16[32,512]{1,0:T(8,128)(2,1)S(1)} %get-tuple-element.9), channel_id=1, source_target_pairs={{0,1},{1,2},{2,3},{3,4},{4,5},{5,6},{6,7},{7,0},{8,9},{9,10},{10,1... | collective-permute-start | bytes 98312 | tf_op jit(solution)/shard_map/ppermute | solution.py:18
  105.6 5.1 %collective-permute-start.5 = (bf16[32,512]{1,0:T(8,128)(2,1)S(1)}, bf16[32,512]{1,0:T(8,128)(2,1)S(1)}, u32[]{:S(2)}, u32[]{:S(2)}) collective-permute-start(bf16[32,512]{1,0:T(8,128)(2,1)S(1)} %get-tuple-element.12), channel_id=1, source_target_pairs={{1,0},{2,1},{3,2},{4,3},{5,4},{6,5},{7,6},{0,7},{9,8},{10,9},{11,1... | collective-permute-start | bytes 98312 | tf_op jit(solution)/shard_map/ppermute | solution.py:19
Sparse Core Ops, SparseCore 0:
  69.6 35.2 reduce-scatter.1
  109.3 41.2 all-reduce.1
where the time goes:
time: 160 us; the launch traced here: 159 us
  waiting for transfers between devices  39.1 us (24%)
  other arithmetic  33.7 us (21%)
  matrix products  27.5 us (17%)
  local copies, waits for them, and re-layouts  24.8 us (16%)
  starting transfers between devices  19.6 us (12%)
  between operations  14.4 us (9%)
    psum x1, waiting for transfers between devices, shards(): share_rows = lax.psum(sector_part, 'band').astype(jnp.float32)  37.5 us
    scatter-add x1, other arithmetic, shards(): jax.ops.segment_sum(grad_inputs[:, feature_width:], edge_dst, num_segment...  10.9 us
    unnamed x42, local copies, waits for them, and re-layouts  10.8 us
    scatter-add x1, other arithmetic, shards(): jax.ops.segment_sum(grad_inputs[:, :feature_width], edge_src, num_segment...  10.7 us
    ppermute x4, starting transfers between devices, with_halo(): before = lax.ppermute(last, axis, up)  10.4 us
    ppermute x4, starting transfers between devices, with_halo(): after = lax.ppermute(initial, axis, down)  9.17 us
    dot_general x1, matrix products, shards(): lax.dot_general(grad_pre_b, w_edge1[feature_width:], (((1,), (1,)), ((),...  6.19 us
    gather x1, local copies, waits for them, and re-layouts, shards(): mesh_table[edge_src]  5.42 us
  transfers between devices with their start and end apart: 10, of which 2 were waited for; matrix products, arithmetic and copies ran while one was open for 26% of the time, Pallas kernels for 0%

commit v1 on v0

v1 whole, which is shorter than its diff:
```python
import functools
import math

import jax
import jax.numpy as jnp
from jax import lax
from jax.experimental import pallas as pl
from jax.experimental.pallas import tpu as pltpu
from jax.sharding import PartitionSpec as P

EPSILON = 1e-05
MESH_ID = pl.DeviceIdType.MESH
F32 = jnp.float32
BF16 = jnp.bfloat16
VMEM_SPEC = pl.BlockSpec(memory_space=pltpu.VMEM)


def dot(a, b):
    return jnp.dot(a, b, preferred_element_type=F32)


def dot_t(a, b):
    return lax.dot_general(a, b, (((1,), (1,)), ((), ())), preferred_element_type=F32)


def t_dot(a, b):
    return lax.dot_general(a, b, (((0,), (0,)), ((), ())), preferred_element_type=F32)


def onehot_rows(index_row, count):
    width = index_row.shape[1]
    return (lax.broadcasted_iota(jnp.int32, (count, width), 0) == index_row).astype(F32).astype(BF16)


def neighbours():
    sectors, bands = lax.axis_size("sector"), lax.axis_size("band")
    s, b = lax.axis_index("sector"), lax.axis_index("band")
    below = {"sector": lax.rem(s + sectors - 1, sectors)}
    above = {"sector": lax.rem(s + 1, sectors)}
    band_below = {"band": lax.rem(b + bands - 1, bands)}
    band_above = {"band": lax.rem(b + 1, bands)}
    return below, above, band_below, band_above


def halo_kernel(mesh_ref, send_ref, out_ref, picked, landed, send_sem, recv_sem):
    below, above, band_below, band_above = neighbours()
    barrier = pltpu.get_barrier_semaphore()
    for other in (below, above, band_below, band_above):
        pl.semaphore_signal(barrier, inc=1, device_id=other, device_id_type=MESH_ID)
    margin = out_ref.shape[1]
    sel = onehot_rows(send_ref[...], mesh_ref.shape[0])
    rows = t_dot(sel, mesh_ref[...]).astype(BF16)
    for g in range(4):
        picked[g] = rows[g * margin : (g + 1) * margin]
    pl.semaphore_wait(barrier, 4)
    copies = []
    for g, (other, slot) in enumerate(((below, 1), (above, 0), (band_below, 3), (band_above, 2))):
        copy = pltpu.make_async_remote_copy(
            src_ref=picked.at[g],
            dst_ref=landed.at[slot],
            send_sem=send_sem.at[g],
            recv_sem=recv_sem.at[slot],
            device_id=other,
            device_id_type=MESH_ID,
        )
        copy.start()
        copies.append(copy)
    for copy in copies:
        copy.wait()
    out_ref[...] = landed[...]


def halo_exchange(mesh_lat, send_row):
    feature = mesh_lat.shape[1]
    margin = send_row.shape[1] // 4
    return pl.pallas_call(
        halo_kernel,
        out_shape=jax.ShapeDtypeStruct((4, margin, feature), BF16),
        in_specs=[VMEM_SPEC] * 2,
        out_specs=VMEM_SPEC,
        scratch_shapes=[
            pltpu.VMEM((4, margin, feature), BF16),
            pltpu.VMEM((4, margin, feature), BF16),
            pltpu.SemaphoreType.DMA((4,)),
            pltpu.SemaphoreType.DMA((4,)),
        ],
        compiler_params=pltpu.CompilerParams(collective_id=0, has_side_effects=True),
    )(mesh_lat, send_row)


def sigmoid(v):
    return jax.nn.sigmoid(v)


def compute_kernel(
    src_ref, dst_ref, grid_ref, own_ref, halo_ref, edge_ref, w1_ref, w2_ref, eg_ref,
    n1_ref, n2_ref, ng_ref, cot_ref,
    out_ref, gg_ref, gto_ref, gth_ref, dw_ref,
    table, proj, sel_t, sel, dsw, xhat, rstd, msg, dagg, tail, gp, red,
    *, edge_block, node_block,
):
    edges, width = edge_ref.shape
    points = grid_ref.shape[0]
    own = own_ref.shape[0]
    rows = own + halo_ref.shape[0]
    table[:own, :] = own_ref[...]
    table[own:, :] = halo_ref[...]
    proj[:rows, :] = dot(table[...], w1_ref[width : 2 * width, :]).astype(BF16)
    proj[rows:, :] = dot(grid_ref[...], w1_ref[2 * width :, :]).astype(BF16)

    def column_onehot(index_row, count):
        columns = jnp.broadcast_to(index_row, (128, index_row.shape[1])).T
        lanes = lax.broadcasted_iota(jnp.int32, columns.shape, 1)
        return [(columns == lanes + k).astype(F32).astype(BF16) for k in range(0, count, 128)]

    def forward(i, carry):
        at = pl.ds(pl.multiple_of(i * edge_block, edge_block), edge_block)
        src, dst = src_ref[:, at], dst_ref[:, at]
        sel_t[:rows, at] = onehot_rows(src, rows)
        sel_t[rows:, at] = onehot_rows(dst, points)
        both = jnp.concatenate(column_onehot(src, rows) + column_onehot(dst, points), axis=1)
        sel[at, :] = both
        pre = dot(edge_ref[at, :], w1_ref[:width, :]) + dot(both, proj[...])
        sig = sigmoid(pre)
        dsw[at, :] = sig * (1.0 + pre * (1.0 - sig))
        raw = dot((pre * sig).astype(BF16), w2_ref[...])
        centred = raw - jnp.mean(raw, axis=-1, keepdims=True)
        scale = lax.rsqrt(jnp.mean(centred * centred, axis=-1, keepdims=True) + EPSILON)
        normed = centred * scale
        xhat[at, :] = normed
        rstd[at, :] = jnp.broadcast_to(scale, (edge_block, 128))
        msg[at, :] = (normed * eg_ref[...]).astype(BF16)
        return carry

    lax.fori_loop(0, edges // edge_block, forward, 0)

    def nodes(i, carry):
        start = pl.multiple_of(i * node_block, node_block)
        at = pl.ds(start, node_block)
        agg = dot(sel_t[pl.ds(rows + start, node_block), :], msg[...]).astype(BF16)
        grid = grid_ref[at, :]
        pre = dot(agg, n1_ref[:width, :]) + dot(grid, n1_ref[width:, :])
        sig = sigmoid(pre)
        raw = dot((pre * sig).astype(BF16), n2_ref[...])
        centred = raw - jnp.mean(raw, axis=-1, keepdims=True)
        scale = lax.rsqrt(jnp.mean(centred * centred, axis=-1, keepdims=True) + EPSILON)
        normed = centred * scale
        out_ref[at, :] = (grid.astype(F32) + normed * ng_ref[...]).astype(BF16)
        cot = cot_ref[at, :].astype(F32)
        dnorm = cot * ng_ref[...]
        draw = scale * (
            dnorm
            - jnp.mean(dnorm, axis=-1, keepdims=True)
            - normed * jnp.mean(dnorm * normed, axis=-1, keepdims=True)
        )
        dhid = dot_t(draw.astype(BF16), n2_ref[...]).astype(BF16).astype(F32)
        dpre = (dhid * (sig * (1.0 + pre * (1.0 - sig)))).astype(BF16)
        dagg[at, :] = dot_t(dpre, n1_ref[:width, :]).astype(BF16)
        tail[at, :] = cot + dot_t(dpre, n1_ref[width:, :]).astype(BF16).astype(F32)
        return carry

    lax.fori_loop(0, points // node_block, nodes, 0)

    def backward(i, carry):
        at = pl.ds(pl.multiple_of(i * edge_block, edge_block), edge_block)
        dnorm = dot(sel[at, rows:], dagg[...]) * eg_ref[...]
        normed = xhat[at, :]
        draw = rstd[at, :1] * (
            dnorm
            - jnp.mean(dnorm, axis=-1, keepdims=True)
            - normed * jnp.mean(dnorm * normed, axis=-1, keepdims=True)
        )
        dhid = dot_t(draw.astype(BF16), w2_ref[...]).astype(BF16).astype(F32)
        gp[at, :] = (dhid * dsw[at, :]).astype(BF16)
        return carry

    lax.fori_loop(0, edges // edge_block, backward, 0)

    grads = gp[...]
    red[...] = dot(sel_t[...], grads).astype(BF16)
    dw_ref[:width, :] = t_dot(edge_ref[...], grads).astype(BF16)
    red_table, red_grid = red[:rows, :], red[rows:, :]
    dw_ref[width : 2 * width, :] = t_dot(table[...], red_table).astype(BF16)
    dw_ref[2 * width :, :] = t_dot(grid_ref[...], red_grid).astype(BF16)
    grad_table = dot_t(red_table, w1_ref[width : 2 * width, :])
    gto_ref[...] = grad_table[:own]
    gth_ref[...] = grad_table[own:].astype(BF16)
    gg_ref[...] = (tail[...] + dot_t(red_grid, w1_ref[2 * width :, :])).astype(BF16)


def local_compute(src, dst, grid, own, halo, edge, w1, w2, eg, n1, n2, ng, cot):
    edges, width = edge.shape
    points = grid.shape[0]
    rows = own.shape[0] + halo.shape[0]
    edge_block = math.gcd(edges, 256)
    node_block = math.gcd(points, 256)
    return pl.pallas_call(
        functools.partial(compute_kernel, edge_block=edge_block, node_block=node_block),
        out_shape=(
            jax.ShapeDtypeStruct((points, width), BF16),
            jax.ShapeDtypeStruct((points, width), BF16),
            jax.ShapeDtypeStruct(own.shape, F32),
            jax.ShapeDtypeStruct(halo.shape, BF16),
            jax.ShapeDtypeStruct(w1.shape, BF16),
        ),
        in_specs=[VMEM_SPEC] * 13,
        out_specs=(VMEM_SPEC,) * 5,
        scratch_shapes=[
            pltpu.VMEM((rows, width), BF16),
            pltpu.VMEM((rows + points, width), BF16),
            pltpu.VMEM((rows + points, edges), BF16),
            pltpu.VMEM((edges, rows + points), BF16),
            pltpu.VMEM((edges, width), F32),
            pltpu.VMEM((edges, width), F32),
            pltpu.VMEM((edges, 128), F32),
            pltpu.VMEM((edges, width), BF16),
            pltpu.VMEM((points, width), BF16),
            pltpu.VMEM((points, width), F32),
            pltpu.VMEM((edges, width), BF16),
            pltpu.VMEM((rows + points, width), BF16),
        ],
        compiler_params=pltpu.CompilerParams(vmem_limit_bytes=60 * 1024 * 1024),
    )(src, dst, grid, own, halo, edge, w1, w2, eg, n1, n2, ng, cot)


def reduce_kernel(
    dw_ref, gth_ref, gto_ref, send_ref, gw_ref, gm_ref,
    r0, a0, r1, a1, r2, fin, r3, ret,
    s0, v0, s1, v1, s2, v2, s3, v3, sh, vh,
    *, grad_scale,
):
    chunks, chips, bands, share, wide = r0.shape
    sectors = 2 * chips
    s, b = lax.axis_index("sector"), lax.axis_index("band")
    core, chip = lax.rem(s, 2), lax.div(s, 2)
    partner = {"sector": s + 1 - 2 * core}
    other_side = {"sector": lax.rem(s + 2 * core - 1 + sectors, sectors)}
    below, above, band_below, band_above = neighbours()
    band_at = [lax.rem(b + o, bands) for o in range(bands)]
    chip_at = [lax.rem(chip + o, chips) for o in range(chips)]
    band_dev = [{"band": band_at[o]} for o in range(1, bands)]
    chip_dev = [{"sector": 2 * chip_at[o] + core} for o in range(1, chips)]

    barrier = pltpu.get_barrier_semaphore()
    peers = [partner, other_side] + band_dev + chip_dev
    for other in peers:
        pl.semaphore_signal(barrier, inc=1, device_id=other, device_id_type=MESH_ID)
    pl.semaphore_wait(barrier, len(peers))

    pending = []

    def send(src, dst, send_sem, recv_sem, other):
        copy = pltpu.make_async_remote_copy(
            src_ref=src, dst_ref=dst, send_sem=send_sem, recv_sem=recv_sem,
            device_id=other, device_id_type=MESH_ID,
        )
        copy.start()
        pending.append(copy)
        return copy

    def cols(c):
        return pl.ds(c * wide, wide)

    first = [
        send(dw_ref.at[:, 1 - core, :, :, cols(c)], r0.at[c], s0.at[c], v0.at[c], partner)
        for c in range(chunks)
    ]
    halos = [
        send(gth_ref.at[g], ret.at[slot], sh.at[g], vh.at[slot], other)
        for g, (other, slot) in enumerate(
            ((below, 1), (above, 0), (band_below, 3), (band_above, 2))
        )
    ]
    second = []
    for c in range(chunks):
        first[c].wait_recv()
        for o in list(range(1, bands)) + [0]:
            at = band_at[o]
            mine = dw_ref[:, core, at, :, c * wide : (c + 1) * wide].astype(F32)
            a0[c, at] = (mine + r0[c, :, at].astype(F32)).astype(BF16)
            if o:
                second.append(
                    send(a0.at[c, at], r1.at[c, o - 1], s1.at[c, o - 1], v1.at[c, o - 1], band_dev[o - 1])
                )
    for copy in halos:
        copy.wait_recv()
    own = gm_ref.shape[0]
    returned = ret[...].reshape(4 * ret.shape[1], ret.shape[2])
    gm_ref[...] = (gto_ref[...] + dot(onehot_rows(send_ref[...], own), returned)).astype(BF16)

    third = []
    for c in range(chunks):
        total = a0[c, b].astype(F32)
        for o in range(1, bands):
            second[c * (bands - 1) + o - 1].wait_recv()
            total = total + r1[c, o - 1].astype(F32)
        a1[c] = total.astype(BF16)
        for o in range(1, chips):
            third.append(
                send(a1.at[c, chip_at[o]], r2.at[c, o - 1], s2.at[c, o - 1], v2.at[c, o - 1], chip_dev[o - 1])
            )
    last = []
    for c in range(chunks):
        total = a1[c, chip].astype(F32)
        for o in range(1, chips):
            third[c * (chips - 1) + o - 1].wait_recv()
            total = total + r2[c, o - 1].astype(F32)
        fin[c] = total.astype(BF16)
        for o in range(1, bands):
            last.append(
                send(fin.at[c], r3.at[c, o - 1], s3.at[c, o - 1], v3.at[c, o - 1], band_dev[o - 1])
            )
        gw_ref[b, :, c * wide : (c + 1) * wide] = fin[c].astype(F32) * grad_scale
    for c in range(chunks):
        for o in range(1, bands):
            last[c * (bands - 1) + o - 1].wait_recv()
            origin = lax.rem(b + bands - o, bands)
            gw_ref[origin, :, c * wide : (c + 1) * wide] = r3[c, o - 1].astype(F32) * grad_scale
    for copy in pending:
        copy.wait_send()


def reduce_gradients(dw, gth, gto, send_row, grad_scale):
    chips, _, bands, share, width = dw.shape
    margin = gth.shape[1]
    chunks = width // math.gcd(width, 256)
    wide = width // chunks
    dma = pltpu.SemaphoreType.DMA
    return pl.pallas_call(
        functools.partial(reduce_kernel, grad_scale=grad_scale),
        out_shape=(
            jax.ShapeDtypeStruct((bands, share, width), F32),
            jax.ShapeDtypeStruct(gto.shape, BF16),
        ),
        in_specs=[VMEM_SPEC] * 4,
        out_specs=(VMEM_SPEC,) * 2,
        scratch_shapes=[
            pltpu.VMEM((chunks, chips, bands, share, wide), BF16),
            pltpu.VMEM((chunks, bands, chips, share, wide), BF16),
            pltpu.VMEM((chunks, bands - 1, chips, share, wide), BF16),
            pltpu.VMEM((chunks, chips, share, wide), BF16),
            pltpu.VMEM((chunks, chips - 1, share, wide), BF16),
            pltpu.VMEM((chunks, share, wide), BF16),
            pltpu.VMEM((chunks, bands - 1, share, wide), BF16),
            pltpu.VMEM((4, margin, width), BF16),
            dma((chunks,)), dma((chunks,)),
            dma((chunks, bands - 1)), dma((chunks, bands - 1)),
            dma((chunks, chips - 1)), dma((chunks, chips - 1)),
            dma((chunks, bands - 1)), dma((chunks, bands - 1)),
            dma((4,)), dma((4,)),
        ],
        compiler_params=pltpu.CompilerParams(
            collective_id=1, has_side_effects=True, vmem_limit_bytes=60 * 1024 * 1024
        ),
    )(dw, gth, gto, send_row)


def shards(
    grid_lat, mesh_lat, edge_feat, edge_src, edge_dst, send_rows,
    w_edge1, w_edge2, edge_gain, w_node1, w_node2, node_gain, cotangent,
):
    width = w_edge2.shape[0]
    lat_rows, lon_cols = grid_lat.shape[:2]
    points = lat_rows * lon_cols
    bands, sectors = lax.axis_size("band"), lax.axis_size("sector")
    margin = send_rows.shape[0] // 4
    send_row = send_rows.reshape(1, -1)
    halo = halo_exchange(mesh_lat, send_row)
    out, gg, gto, gth, dw = local_compute(
        edge_src.reshape(1, -1),
        edge_dst.reshape(1, -1),
        grid_lat.reshape(points, width),
        mesh_lat,
        halo.reshape(4 * margin, width),
        edge_feat,
        w_edge1,
        w_edge2,
        edge_gain.reshape(1, -1),
        w_node1,
        w_node2,
        node_gain.reshape(1, -1),
        cotangent.reshape(points, width),
    )
    total_edges = edge_feat.shape[0] * bands * sectors
    share = w_edge1.shape[0] // (bands * sectors)
    gw, gm = reduce_gradients(
        dw.reshape(sectors // 2, 2, bands, share, width),
        gth.reshape(4, margin, width),
        gto,
        send_row,
        1.0 / math.sqrt(total_edges),
    )
    return (
        out.reshape(lat_rows, lon_cols, width),
        gg.reshape(lat_rows, lon_cols, width),
        gm,
        gw.reshape(bands * share, width),
    )


def solution(mesh):
    in_specs = (
        P("band", "sector", None),
        P(("band", "sector"), None),
        P(("band", "sector"), None),
        P(("band", "sector")),
        P(("band", "sector")),
        P(("band", "sector")),
        P(),
        P(),
        P(),
        P(),
        P(),
        P(),
        P("band", "sector", None),
    )
    out_specs = (
        P("band", "sector", None),
        P("band", "sector", None),
        P(("band", "sector"), None),
        P("sector", None),
    )
    return jax.shard_map(shards, mesh=mesh, in_specs=in_specs, out_specs=out_specs, check_vma=False)
```

time: 160 us -> 64.5 us (0.40)
  Pallas kernels: 0 us -> 57.6 us
  waiting for transfers between devices: 39.1 us -> 0 us
  other arithmetic: 33.7 us -> 0 us
  matrix products: 27.5 us -> 0 us
  starting transfers between devices: 19.6 us -> 0 us
  local copies, waits for them, and re-layouts: 24.8 us -> 5.92 us
  between operations: 14.4 us -> 0.65 us
    pallas_call x0 -> x3, Pallas kernels: none -> 57.6 us  [the longest x1 24.2 us: reduce_gradients(): pl.pallas_call(functools.partial(reduce_kernel, grad_scale=grad_scale), o...]
    psum x1 -> x0, waiting for transfers between devices: 37.5 us -> none  [shards(): share_rows = lax.psum(sector_part, 'band').astype(jnp.float32)]
    dot_general x10 -> x0, matrix products: 27.5 us -> none  [the longest x1 6.19 us: shards(): lax.dot_general(grad_pre_b, w_edge1[feature_width:], (((1,), (1,)), ((),...]
    scatter-add x3 -> x0, other arithmetic: 23.1 us -> none  [the longest x1 10.9 us: shards(): jax.ops.segment_sum(grad_inputs[:, feature_width:], edge_dst, num_segment...]
    ppermute x8 -> x0, starting transfers between devices: 19.5 us -> none  [the longest x4 10.4 us: with_halo(): before = lax.ppermute(last, axis, up)]
    gather x3 -> x0, local copies, waits for them, and re-layouts: 12 us -> none  [the longest x1 5.42 us: shards(): mesh_table[edge_src]]
    unnamed x42 -> x2, local copies, waits for them, and re-layouts: 10.8 us -> 3.33 us
    reduce_sum x4 -> x0, other arithmetic: 3.05 us -> none  [the longest x2 2.23 us: layer_norm(): centred = values - average]
  transfers between devices with their start and end apart: 10 -> 0, of which waited for: 2 -> 0; matrix products, arithmetic and copies ran while one was open for 26% -> 0% of each run, Pallas kernels for 0% -> 0%
where the time goes in v1:
time: 64.5 us; the launch traced here: 64.2 us
  Pallas kernels  57.6 us (89%)
  local copies, waits for them, and re-layouts  5.92 us (9%)
  between operations  0.65 us (1%)
    pallas_call x1, Pallas kernels, reduce_gradients(): pl.pallas_call(functools.partial(reduce_kernel, grad_scale=grad_scale), o...  24.2 us
    pallas_call x1, Pallas kernels, local_compute(): pl.pallas_call(functools.partial(compute_kernel, edge_block=edge_block, n...  22.5 us
    pallas_call x1, Pallas kernels, halo_exchange(): pl.pallas_call(halo_kernel, out_shape=jax.ShapeDtypeStruct((4, margin, fe...  10.8 us
    unnamed x2, local copies, waits for them, and re-layouts  3.33 us
    reshape x1, local copies, waits for them, and re-layouts, shards(): edge_src.reshape(1, -1)  1.29 us
    reshape x1, local copies, waits for them, and re-layouts, shards(): edge_dst.reshape(1, -1)  1.29 us

profile of v1, /device:TPU:0, one launch (start us, length us, event | category | flops | bytes accessed | tf_op | source)
XLA Modules:
  0.0 64.2 jit_solution(11726245103654817695)
XLA Ops:
  0.6 1.3 %reshape.47.src_ref = s32[1,1536]{1,0:T(1,128)} reshape(s32[1536]{0:T(1024)} %param.16) | data formatting | bytes 12288 | tf_op jit(solution)/shard_map/reshape | solution.py:370
  1.9 1.3 %reshape.48.dst_ref = s32[1,1536]{1,0:T(1,128)} reshape(s32[1536]{0:T(1024)} %param.17) | data formatting | bytes 12288 | tf_op jit(solution)/shard_map/reshape | solution.py:371
  3.2 10.8 %shard_map.156 = bf16[4,32,512]{2,1,0:T(8,128)(2,1)} custom-call(bf16[128,512]{1,0:T(8,128)(2,1)} %own_ref.1, s32[1,128]{1,0:T(1,128)} %bitcast.19), custom_call_target="tpu_custom_call" | custom-call | tf_op jit(solution)/shard_map/pallas_call | solution.py:76
  14.1 22.5 %shard_map.157 = (bf16[512,512]{1,0:T(8,128)(2,1)}, bf16[512,512]{1,0:T(8,128)(2,1)}, f32[128,512]{1,0:T(8,128)}, bf16[128,512]{1,0:T(8,128)(2,1)}, bf16[1536,512]{1,0:T(8,128)(2,1)}) custom-call(s32[1,1536]{1,0:T(1,128)} %reshape.47.src_ref, s32[1,1536]{1,0:T(1,128)} %reshape.48.dst_ref, bf16[512,512]{1,0:T(8,128)(2,1)} %bitcast.12, ...), custom_call_target="tpu_custom_call" | custom-call | tf_op jit(solution)/shard_map/pallas_call | solution.py:197
  36.6 24.2 %shard_map.158 = (f32[4,48,512]{2,1,0:T(8,128)}, bf16[128,512]{1,0:T(8,128)(2,1)}) custom-call(bf16[4,2,4,48,512]{4,3,2,1,0:T(8,128)(2,1)} %bitcast.11, bf16[4,32,512]{2,1,0:T(8,128)(2,1)} %bitcast.16, f32[128,512]{1,0:T(8,128)} %get-tuple-element.15.gto_ref, s32[1,128]{1,0:T(1,128)} %bitcast.20), custom_call_target="tpu_custom_call" | custom-call | tf_op jit(solution)/shard_map/pallas_call | solution.py:329
  60.9 1.6 %copy.19 = bf16[128,512]{1,0:T(8,128)(2,1)} copy(bf16[128,512]{1,0:T(8,128)(2,1)} %get-tuple-element.24) | data formatting | bytes 262144
  62.4 1.8 %copy.20 = f32[192,512]{1,0:T(8,128)} copy(f32[192,512]{1,0:T(8,128)} %bitcast.15) | data formatting | bytes 786432

commit v2 on v1

v2 whole, which is shorter than its diff:
```python
import functools
import math

import jax
import jax.numpy as jnp
from jax import lax
from jax.experimental import pallas as pl
from jax.experimental.pallas import tpu as pltpu
from jax.sharding import PartitionSpec as P

EPSILON = 1e-05
MESH_ID = pl.DeviceIdType.MESH
F32 = jnp.float32
BF16 = jnp.bfloat16
VMEM_SPEC = pl.BlockSpec(memory_space=pltpu.VMEM)


def dot(a, b):
    return jnp.dot(a, b, preferred_element_type=F32)


def dot_t(a, b):
    return lax.dot_general(a, b, (((1,), (1,)), ((), ())), preferred_element_type=F32)


def t_dot(a, b):
    return lax.dot_general(a, b, (((0,), (0,)), ((), ())), preferred_element_type=F32)


def onehot_rows(index_row, count):
    width = index_row.shape[1]
    return (lax.broadcasted_iota(jnp.int32, (count, width), 0) == index_row).astype(F32).astype(BF16)


def neighbours():
    sectors, bands = lax.axis_size("sector"), lax.axis_size("band")
    s, b = lax.axis_index("sector"), lax.axis_index("band")
    below = {"sector": lax.rem(s + sectors - 1, sectors)}
    above = {"sector": lax.rem(s + 1, sectors)}
    band_below = {"band": lax.rem(b + bands - 1, bands)}
    band_above = {"band": lax.rem(b + 1, bands)}
    return below, above, band_below, band_above


def sigmoid(v):
    return jax.nn.sigmoid(v)


def layer_stats(raw):
    centred = raw - jnp.mean(raw, axis=-1, keepdims=True)
    scale = lax.rsqrt(jnp.mean(centred * centred, axis=-1, keepdims=True) + EPSILON)
    return centred * scale, scale


def layer_back(dnorm, normed, scale):
    return scale * (
        dnorm
        - jnp.mean(dnorm, axis=-1, keepdims=True)
        - normed * jnp.mean(dnorm * normed, axis=-1, keepdims=True)
    )


def column_onehot(index_row, count):
    columns = jnp.broadcast_to(index_row, (128, index_row.shape[1])).T
    lanes = lax.broadcasted_iota(jnp.int32, columns.shape, 1)
    return [(columns == lanes + k).astype(F32).astype(BF16) for k in range(0, count, 128)]


def step_kernel(
    src_ref, dst_ref, send_ref, own_ref, eg_ref, ng_ref,
    w1_hbm, grid_hbm, edge_hbm, w2_hbm, n1_hbm, n2_hbm, cot_hbm,
    out_ref, gg_ref, gm_ref, gw_ref,
    w1_ref, grid_ref, edge_ref, w2_ref, n1_ref, n2_ref, cot_ref, load_sem,
    picked, landed, hs, hv,
    table, proj, sel_t, sel, dsw, xhat, rstd, msg, dagg, tail, gp, red,
    dw, r0, a0, r1, a1, r2, fin, r3, gth, ret,
    s0, v0, s1, v1, s2, v2, s3, v3, sh, vh,
    *, edge_block, node_block,
):
    chunks, chips, bands, share, wide = r0.shape
    sectors = 2 * chips
    s, b = lax.axis_index("sector"), lax.axis_index("band")
    core, chip = lax.rem(s, 2), lax.div(s, 2)
    partner = {"sector": s + 1 - 2 * core}
    other_side = {"sector": lax.rem(s + 2 * core - 1 + sectors, sectors)}
    below, above, band_below, band_above = neighbours()
    band_at = [lax.rem(b + o, bands) for o in range(bands)]
    chip_at = [lax.rem(chip + o, chips) for o in range(chips)]
    band_dev = [{"band": band_at[o]} for o in range(1, bands)]
    chip_dev = [{"sector": 2 * chip_at[o] + core} for o in range(1, chips)]
    routes = ((below, 1), (above, 0), (band_below, 3), (band_above, 2))

    barrier = pltpu.get_barrier_semaphore()
    peers = [partner, other_side] + band_dev + chip_dev
    for other in peers:
        pl.semaphore_signal(barrier, inc=1, device_id=other, device_id_type=MESH_ID)

    loads = []
    pairs = (
        (w1_hbm, w1_ref), (grid_hbm, grid_ref), (edge_hbm, edge_ref), (w2_hbm, w2_ref),
        (n1_hbm, n1_ref), (n2_hbm, n2_ref), (cot_hbm, cot_ref),
    )
    for k, (far, near) in enumerate(pairs):
        load = pltpu.make_async_copy(far, near, load_sem.at[k])
        load.start()
        loads.append(load)

    pending = []

    def send(src, dst, send_sem, recv_sem, other):
        copy = pltpu.make_async_remote_copy(
            src_ref=src, dst_ref=dst, send_sem=send_sem, recv_sem=recv_sem,
            device_id=other, device_id_type=MESH_ID,
        )
        copy.start()
        pending.append(copy)
        return copy

    edges, width = edge_ref.shape
    points = grid_ref.shape[0]
    own = own_ref.shape[0]
    margin = picked.shape[1]
    rows = own + 4 * margin
    send_sel = onehot_rows(send_ref[...], own)
    chosen = t_dot(send_sel, own_ref[...]).astype(BF16)
    for g in range(4):
        picked[g] = chosen[g * margin : (g + 1) * margin]
    pl.semaphore_wait(barrier, len(peers))
    halos = [
        send(picked.at[g], landed.at[slot], hs.at[g], hv.at[slot], other)
        for g, (other, slot) in enumerate(routes)
    ]

    loads[0].wait()
    loads[1].wait()
    proj[rows:, :] = dot(grid_ref[...], w1_ref[2 * width :, :]).astype(BF16)
    loads[2].wait()

    def prepare(i, carry):
        at = pl.ds(pl.multiple_of(i * edge_block, edge_block), edge_block)
        src = src_ref[at].reshape(1, edge_block)
        dst = dst_ref[at].reshape(1, edge_block)
        sel_t[:rows, at] = onehot_rows(src, rows)
        sel_t[rows:, at] = onehot_rows(dst, points)
        sel[at, :rows] = jnp.concatenate(column_onehot(src, rows), axis=1)
        to_grid = jnp.concatenate(column_onehot(dst, points), axis=1)
        sel[at, rows:] = to_grid
        dsw[at, :] = dot(edge_ref[at, :], w1_ref[:width, :]) + dot(to_grid, proj[rows:, :])
        return carry

    lax.fori_loop(0, edges // edge_block, prepare, 0)

    for copy in halos:
        copy.wait_recv()
    table[:own, :] = own_ref[...]
    for g in range(4):
        table[own + g * margin : own + (g + 1) * margin, :] = landed[g]
    proj[:rows, :] = dot(table[...], w1_ref[width : 2 * width, :]).astype(BF16)
    loads[3].wait()

    def forward(i, carry):
        at = pl.ds(pl.multiple_of(i * edge_block, edge_block), edge_block)
        pre = dsw[at, :] + dot(sel[at, :rows], proj[:rows, :])
        sig = sigmoid(pre)
        dsw[at, :] = sig * (1.0 + pre * (1.0 - sig))
        normed, scale = layer_stats(dot((pre * sig).astype(BF16), w2_ref[...]))
        xhat[at, :] = normed
        rstd[at, :] = jnp.broadcast_to(scale, (edge_block, 128))
        msg[at, :] = (normed * eg_ref[...]).astype(BF16)
        return carry

    lax.fori_loop(0, edges // edge_block, forward, 0)
    for load in loads[4:]:
        load.wait()

    def nodes(i, carry):
        start = pl.multiple_of(i * node_block, node_block)
        at = pl.ds(start, node_block)
        agg = dot(sel_t[pl.ds(rows + start, node_block), :], msg[...]).astype(BF16)
        grid = grid_ref[at, :]
        pre = dot(agg, n1_ref[:width, :]) + dot(grid, n1_ref[width:, :])
        sig = sigmoid(pre)
        normed, scale = layer_stats(dot((pre * sig).astype(BF16), n2_ref[...]))
        out_ref[at, :] = (grid.astype(F32) + normed * ng_ref[...]).astype(BF16)
        cot = cot_ref[at, :].astype(F32)
        draw = layer_back(cot * ng_ref[...], normed, scale)
        dhid = dot_t(draw.astype(BF16), n2_ref[...]).astype(BF16).astype(F32)
        dpre = (dhid * (sig * (1.0 + pre * (1.0 - sig)))).astype(BF16)
        dagg[at, :] = dot_t(dpre, n1_ref[:width, :]).astype(BF16)
        tail[at, :] = cot + dot_t(dpre, n1_ref[width:, :]).astype(BF16).astype(F32)
        return carry

    lax.fori_loop(0, points // node_block, nodes, 0)

    def backward(i, carry):
        at = pl.ds(pl.multiple_of(i * edge_block, edge_block), edge_block)
        dnorm = dot(sel[at, rows:], dagg[...]) * eg_ref[...]
        draw = layer_back(dnorm, xhat[at, :], rstd[at, :1])
        dhid = dot_t(draw.astype(BF16), w2_ref[...]).astype(BF16).astype(F32)
        gp[at, :] = (dhid * dsw[at, :]).astype(BF16)
        return carry

    lax.fori_loop(0, edges // edge_block, backward, 0)

    def put(c, start, value):
        stop = start + value.shape[0]
        for k in range(start // share, -(-stop // share)):
            low, high = max(k * share, start), min((k + 1) * share, stop)
            at = (k // bands // 2, k // bands % 2, k % bands)
            piece = value[low - start : high - start].astype(BF16)
            dw[c, at[0], at[1], at[2], low - k * share : high - k * share] = piece

    first, second, third, last = [], [], [], []

    def band_stage(c):
        first[c].wait_recv()
        for o in list(range(1, bands)) + [0]:
            at = band_at[o]
            mine = dw[c, :, core, at].astype(F32)
            a0[c, at] = (mine + r0[c, :, at].astype(F32)).astype(BF16)
            if o:
                second.append(
                    send(a0.at[c, at], r1.at[c, o - 1], s1.at[c, o - 1], v1.at[c, o - 1], band_dev[o - 1])
                )

    for c in range(chunks):
        low, high = c * wide, (c + 1) * wide
        grads = gp[:, low:high]
        put(c, 0, t_dot(edge_ref[...], grads))
        part = dot(sel_t[...], grads).astype(BF16)
        red[:, low:high] = part
        put(c, width, t_dot(table[...], part[:rows]))
        put(c, 2 * width, t_dot(grid_ref[...], part[rows:]))
        first.append(send(dw.at[c, :, 1 - core], r0.at[c], s0.at[c], v0.at[c], partner))
        if c:
            band_stage(c - 1)
    grad_table = dot_t(red[:rows, :], w1_ref[width : 2 * width, :])
    for g in range(4):
        gth[g] = grad_table[own + g * margin : own + (g + 1) * margin].astype(BF16)
    backs = [
        send(gth.at[g], ret.at[slot], sh.at[g], vh.at[slot], other)
        for g, (other, slot) in enumerate(routes)
    ]
    band_stage(chunks - 1)
    gg_ref[...] = (tail[...] + dot_t(red[rows:, :], w1_ref[2 * width :, :])).astype(BF16)
    for copy in backs:
        copy.wait_recv()
    returned = ret[...].reshape(4 * margin, width)
    gm_ref[...] = (grad_table[:own] + dot(send_sel, returned)).astype(BF16)

    for c in range(chunks):
        total = a0[c, b].astype(F32)
        for o in range(1, bands):
            second[c * (bands - 1) + o - 1].wait_recv()
            total = total + r1[c, o - 1].astype(F32)
        a1[c] = total.astype(BF16)
        for o in range(1, chips):
            third.append(
                send(a1.at[c, chip_at[o]], r2.at[c, o - 1], s2.at[c, o - 1], v2.at[c, o - 1], chip_dev[o - 1])
            )
    for c in range(chunks):
        total = a1[c, chip].astype(F32)
        for o in range(1, chips):
            third[c * (chips - 1) + o - 1].wait_recv()
            total = total + r2[c, o - 1].astype(F32)
        fin[c] = total.astype(BF16)
        for o in range(1, bands):
            last.append(
                send(fin.at[c], r3.at[c, o - 1], s3.at[c, o - 1], v3.at[c, o - 1], band_dev[o - 1])
            )
        gw_ref[b, :, c * wide : (c + 1) * wide] = fin[c]
    for c in range(chunks):
        for o in range(1, bands):
            last[c * (bands - 1) + o - 1].wait_recv()
            origin = lax.rem(b + bands - o, bands)
            gw_ref[origin, :, c * wide : (c + 1) * wide] = r3[c, o - 1]
    for copy in pending:
        copy.wait_send()


def finish_kernel(grad_scale, out_in, gg_in, gm_in, gw_in, out_ref, gg_ref, gm_ref, gw_ref):
    out_ref[...] = out_in[...]
    gg_ref[...] = gg_in[...]
    gm_ref[...] = gm_in[...]
    gw_ref[...] = gw_in[...].astype(F32) * grad_scale


def decode_step(src, dst, send_row, own, eg, ng, w1, grid, edge, w2, n1, n2, cot):
    edges, width = edge.shape
    points = grid.shape[0]
    margin = send_row.shape[1] // 4
    rows = own.shape[0] + 4 * margin
    bands, sectors = lax.axis_size("band"), lax.axis_size("sector")
    chips = sectors // 2
    share = w1.shape[0] // (bands * sectors)
    chunks = width // math.gcd(width, 256)
    wide = width // chunks
    dma = pltpu.SemaphoreType.DMA
    whole = (w1, grid, edge, w2, n1, n2, cot)
    results = pl.pallas_call(
        functools.partial(
            step_kernel, edge_block=math.gcd(edges, 256), node_block=math.gcd(points, 256)
        ),
        out_shape=(
            jax.ShapeDtypeStruct((points, width), BF16),
            jax.ShapeDtypeStruct((points, width), BF16),
            jax.ShapeDtypeStruct(own.shape, BF16),
            jax.ShapeDtypeStruct((bands, share, width), BF16),
        ),
        in_specs=[VMEM_SPEC] * 6 + [pl.BlockSpec(memory_space=pl.ANY)] * 7,
        out_specs=(VMEM_SPEC,) * 4,
        scratch_shapes=[pltpu.VMEM(a.shape, a.dtype) for a in whole]
        + [
            dma((len(whole),)),
            pltpu.VMEM((4, margin, width), BF16),
            pltpu.VMEM((4, margin, width), BF16),
            dma((4,)), dma((4,)),
            pltpu.VMEM((rows, width), BF16),
            pltpu.VMEM((rows + points, width), BF16),
            pltpu.VMEM((rows + points, edges), BF16),
            pltpu.VMEM((edges, rows + points), BF16),
            pltpu.VMEM((edges, width), F32),
            pltpu.VMEM((edges, width), F32),
            pltpu.VMEM((edges, 128), F32),
            pltpu.VMEM((edges, width), BF16),
            pltpu.VMEM((points, width), BF16),
            pltpu.VMEM((points, width), F32),
            pltpu.VMEM((edges, width), BF16),
            pltpu.VMEM((rows + points, width), BF16),
            pltpu.VMEM((chunks, chips, 2, bands, share, wide), BF16),
            pltpu.VMEM((chunks, chips, bands, share, wide), BF16),
            pltpu.VMEM((chunks, bands, chips, share, wide), BF16),
            pltpu.VMEM((chunks, bands - 1, chips, share, wide), BF16),
            pltpu.VMEM((chunks, chips, share, wide), BF16),
            pltpu.VMEM((chunks, chips - 1, share, wide), BF16),
            pltpu.VMEM((chunks, share, wide), BF16),
            pltpu.VMEM((chunks, bands - 1, share, wide), BF16),
            pltpu.VMEM((4, margin, width), BF16),
            pltpu.VMEM((4, margin, width), BF16),
            dma((chunks,)), dma((chunks,)),
            dma((chunks, bands - 1)), dma((chunks, bands - 1)),
            dma((chunks, chips - 1)), dma((chunks, chips - 1)),
            dma((chunks, bands - 1)), dma((chunks, bands - 1)),
            dma((4,)), dma((4,)),
        ],
        compiler_params=pltpu.CompilerParams(
            collective_id=0, has_side_effects=True, vmem_limit_bytes=60 * 1024 * 1024
        ),
    )(src, dst, send_row, own, eg, ng, *whole)
    grad_scale = 1.0 / math.sqrt(edges * bands * sectors)
    return pl.pallas_call(
        functools.partial(finish_kernel, grad_scale),
        out_shape=tuple(
            jax.ShapeDtypeStruct(r.shape, F32 if k == 3 else BF16) for k, r in enumerate(results)
        ),
        in_specs=[VMEM_SPEC] * 4,
        out_specs=(VMEM_SPEC,) * 4,
    )(*results)


def shards(
    grid_lat, mesh_lat, edge_feat, edge_src, edge_dst, send_rows,
    w_edge1, w_edge2, edge_gain, w_node1, w_node2, node_gain, cotangent,
):
    width = w_edge2.shape[0]
    lat_rows, lon_cols = grid_lat.shape[:2]
    points = lat_rows * lon_cols
    out, gg, gm, gw = decode_step(
        edge_src,
        edge_dst,
        send_rows.reshape(1, -1),
        mesh_lat,
        edge_gain.reshape(1, -1),
        node_gain.reshape(1, -1),
        w_edge1,
        grid_lat.reshape(points, width),
        edge_feat,
        w_edge2,
        w_node1,
        w_node2,
        cotangent.reshape(points, width),
    )
    return (
        out.reshape(lat_rows, lon_cols, width),
        gg.reshape(lat_rows, lon_cols, width),
        gm,
        gw.reshape(-1, width),
    )


def solution(mesh):
    in_specs = (
        P("band", "sector", None),
        P(("band", "sector"), None),
        P(("band", "sector"), None),
        P(("band", "sector")),
        P(("band", "sector")),
        P(("band", "sector")),
        P(),
        P(),
        P(),
        P(),
        P(),
        P(),
        P("band", "sector", None),
    )
    out_specs = (
        P("band", "sector", None),
        P("band", "sector", None),
        P(("band", "sector"), None),
        P("sector", None),
    )
    return jax.shard_map(shards, mesh=mesh, in_specs=in_specs, out_specs=out_specs, check_vma=False)
```

time: 64.5 us -> 50 us (0.78)
  Pallas kernels: 57.6 us -> 49.2 us
  local copies, waits for them, and re-layouts: 5.92 us -> 0 us
    pallas_call x3 -> x2, Pallas kernels: 57.6 us -> 49.2 us  [the longest x1 46.7 us: decode_step(): pl.pallas_call(functools.partial(step_kernel, edge_block=math.gcd(edges,...]
    unnamed x2 -> x0, local copies, waits for them, and re-layouts: 3.33 us -> none
    reshape x2 -> x0, local copies, waits for them, and re-layouts: 2.59 us -> none  [the longest x1 1.29 us: shards(): edge_src.reshape(1, -1)]
where the time goes in v2:
time: 50 us; the launch traced here: 49.8 us
  Pallas kernels  49.2 us (98%)
  between operations  0.64 us (1%)
    pallas_call x1, Pallas kernels, decode_step(): pl.pallas_call(functools.partial(step_kernel, edge_block=math.gcd(edges,...  46.7 us
    pallas_call x1, Pallas kernels, decode_step(): pl.pallas_call(functools.partial(finish_kernel, grad_scale), out_shape=tu...  2.45 us

profile of v2, /device:TPU:0, one launch (start us, length us, event | category | flops | bytes accessed | tf_op | source)
XLA Modules:
  0.0 49.8 jit_solution(14190572627636920547)
XLA Ops:
  0.6 46.7 %shard_map.156 = (bf16[512,512]{1,0:T(8,128)(2,1)}, bf16[512,512]{1,0:T(8,128)(2,1)}, bf16[128,512]{1,0:T(8,128)(2,1)}, bf16[4,48,512]{2,1,0:T(8,128)(2,1)}) custom-call(s32[1536]{0:T(1024)} %src_ref.1, s32[1536]{0:T(1024)} %dst_ref.1, s32[1,128]{1,0:T(1,128)} %bitcast.12, bf16[128,512]{1,0:T(8,128)(2,1)} %own_ref.1, f32[1,512]{1,0:T(1,128)} %bitcast.10, ...), custom_call_target="tpu_custom_call" | custom-call | tf_op jit(solution)/shard_map/pallas_call | solution.py:300
  47.4 2.5 %shard_map.157 = (bf16[512,512]{1,0:T(8,128)(2,1)}, bf16[512,512]{1,0:T(8,128)(2,1)}, bf16[128,512]{1,0:T(8,128)(2,1)}, f32[4,48,512]{2,1,0:T(8,128)}) custom-call(bf16[512,512]{1,0:T(8,128)(2,1)} %get-tuple-element.12.out_in, bf16[512,512]{1,0:T(8,128)(2,1)} %get-tuple-element.13.gg_in, bf16[128,512]{1,0:T(8,128)(2,1)} %get-tuple-element.14.gm_in, ...), custom_call_target="tpu_custom_call" | custom-call | tf_op jit(solution)/shard_map/pallas_call | solution.py:351

commit v3 on v2

--- a/solution.py
+++ b/solution.py
@@ -10,6 +10,8 @@
 
 EPSILON = 1e-05
 MESH_ID = pl.DeviceIdType.MESH
+LANES = 128
+GROUP = 2
 F32 = jnp.float32
 BF16 = jnp.bfloat16
 VMEM_SPEC = pl.BlockSpec(memory_space=pltpu.VMEM)
@@ -29,7 +31,9 @@
 
 def onehot_rows(index_row, count):
     width = index_row.shape[1]
-    return (lax.broadcasted_iota(jnp.int32, (count, width), 0) == index_row).astype(F32).astype(BF16)
+    rows = lax.broadcasted_iota(jnp.int16, (count, width), 0)
+    hit = rows == jnp.broadcast_to(index_row.astype(jnp.int16), (count, width))
+    return jnp.where(hit, jnp.ones((), BF16), jnp.zeros((), BF16))
 
 
 def neighbours():
@@ -43,7 +47,7 @@
 
 
 def sigmoid(v):
-    return jax.nn.sigmoid(v)
+    return 0.5 * jnp.tanh(0.5 * v) + 0.5
 
 
 def layer_stats(raw):
@@ -62,8 +66,12 @@
 
 def column_onehot(index_row, count):
     columns = jnp.broadcast_to(index_row, (128, index_row.shape[1])).T
-    lanes = lax.broadcasted_iota(jnp.int32, columns.shape, 1)
-    return [(columns == lanes + k).astype(F32).astype(BF16) for k in range(0, count, 128)]
+    columns = columns.astype(jnp.int16)
+    lanes = lax.broadcasted_iota(jnp.int16, columns.shape, 1)
+    one, zero = jnp.ones((), BF16), jnp.zeros((), BF16)
+    return [
+        jnp.where(columns - jnp.int16(k) == lanes, one, zero) for k in range(0, count, 128)
+    ]
 
 
 def step_kernel(
@@ -72,7 +80,7 @@
     out_ref, gg_ref, gm_ref, gw_ref,
     w1_ref, grid_ref, edge_ref, w2_ref, n1_ref, n2_ref, cot_ref, load_sem,
     picked, landed, hs, hv,
-    table, proj, sel_t, sel, dsw, xhat, rstd, msg, dagg, tail, gp, red,
+    table, proj, edge_t, grid_t, table_t, w2_t, sel_t, sel, dsw, xhat, rstd, msg, dagg, tail, gp, red,
     dw, r0, a0, r1, a1, r2, fin, r3, gth, ret,
     s0, v0, s1, v1, s2, v2, s3, v3, sh, vh,
     *, edge_block, node_block,
@@ -134,6 +142,7 @@
     loads[0].wait()
     loads[1].wait()
     proj[rows:, :] = dot(grid_ref[...], w1_ref[2 * width :, :]).astype(BF16)
+    grid_t[...] = grid_ref[...].T
     loads[2].wait()
 
     def prepare(i, carry):
@@ -145,6 +154,7 @@
         sel[at, :rows] = jnp.concatenate(column_onehot(src, rows), axis=1)
         to_grid = jnp.concatenate(column_onehot(dst, points), axis=1)
         sel[at, rows:] = to_grid
+        edge_t[:, at] = edge_ref[at, :].T
         dsw[at, :] = dot(edge_ref[at, :], w1_ref[:width, :]) + dot(to_grid, proj[rows:, :])
         return carry
 
@@ -156,14 +166,17 @@
     for g in range(4):
         table[own + g * margin : own + (g + 1) * margin, :] = landed[g]
     proj[:rows, :] = dot(table[...], w1_ref[width : 2 * width, :]).astype(BF16)
+    table_t[...] = table[...].T
     loads[3].wait()
+    w2_t[...] = w2_ref[...].T
 
     def forward(i, carry):
         at = pl.ds(pl.multiple_of(i * edge_block, edge_block), edge_block)
         pre = dsw[at, :] + dot(sel[at, :rows], proj[:rows, :])
         sig = sigmoid(pre)
-        dsw[at, :] = sig * (1.0 + pre * (1.0 - sig))
-        normed, scale = layer_stats(dot((pre * sig).astype(BF16), w2_ref[...]))
+        act = pre * sig
+        dsw[at, :] = sig + act * (1.0 - sig)
+        normed, scale = layer_stats(dot(act.astype(BF16), w2_ref[...]))
         xhat[at, :] = normed
         rstd[at, :] = jnp.broadcast_to(scale, (edge_block, 128))
         msg[at, :] = (normed * eg_ref[...]).astype(BF16)
@@ -196,7 +209,7 @@
         at = pl.ds(pl.multiple_of(i * edge_block, edge_block), edge_block)
         dnorm = dot(sel[at, rows:], dagg[...]) * eg_ref[...]
         draw = layer_back(dnorm, xhat[at, :], rstd[at, :1])
-        dhid = dot_t(draw.astype(BF16), w2_ref[...]).astype(BF16).astype(F32)
+        dhid = dot(draw.astype(BF16), w2_t[...]).astype(BF16).astype(F32)
         gp[at, :] = (dhid * dsw[at, :]).astype(BF16)
         return carry
 
@@ -208,7 +221,10 @@
             low, high = max(k * share, start), min((k + 1) * share, stop)
             at = (k // bands // 2, k // bands % 2, k % bands)
             piece = value[low - start : high - start].astype(BF16)
-            dw[c, at[0], at[1], at[2], low - k * share : high - k * share] = piece
+            for j in range(value.shape[1] // wide):
+                dw[c + j, at[0], at[1], at[2], low - k * share : high - k * share] = piece[
+                    :, j * wide : (j + 1) * wide
+                ]
 
     first, second, third, last = [], [], [], []
 
@@ -216,24 +232,25 @@
         first[c].wait_recv()
         for o in list(range(1, bands)) + [0]:
             at = band_at[o]
-            mine = dw[c, :, core, at].astype(F32)
-            a0[c, at] = (mine + r0[c, :, at].astype(F32)).astype(BF16)
+            a0[c, at] = dw[c, :, core, at] + r0[c, :, at]
             if o:
                 second.append(
                     send(a0.at[c, at], r1.at[c, o - 1], s1.at[c, o - 1], v1.at[c, o - 1], band_dev[o - 1])
                 )
 
-    for c in range(chunks):
-        low, high = c * wide, (c + 1) * wide
+    group = math.gcd(chunks, GROUP)
+    for c in range(0, chunks, group):
+        low, high = c * wide, (c + group) * wide
         grads = gp[:, low:high]
-        put(c, 0, t_dot(edge_ref[...], grads))
         part = dot(sel_t[...], grads).astype(BF16)
         red[:, low:high] = part
-        put(c, width, t_dot(table[...], part[:rows]))
-        put(c, 2 * width, t_dot(grid_ref[...], part[rows:]))
-        first.append(send(dw.at[c, :, 1 - core], r0.at[c], s0.at[c], v0.at[c], partner))
-        if c:
-            band_stage(c - 1)
+        put(c, 0, dot(edge_t[...], grads))
+        put(c, width, dot(table_t[...], part[:rows]))
+        put(c, 2 * width, dot(grid_t[...], part[rows:]))
+        for j in range(c, c + group):
+            first.append(send(dw.at[j, :, 1 - core], r0.at[j], s0.at[j], v0.at[j], partner))
+        for j in range(max(c - group, 0), c):
+            band_stage(j)
     grad_table = dot_t(red[:rows, :], w1_ref[width : 2 * width, :])
     for g in range(4):
         gth[g] = grad_table[own + g * margin : own + (g + 1) * margin].astype(BF16)
@@ -241,7 +258,8 @@
         send(gth.at[g], ret.at[slot], sh.at[g], vh.at[slot], other)
         for g, (other, slot) in enumerate(routes)
     ]
-    band_stage(chunks - 1)
+    for j in range(chunks - group, chunks):
+        band_stage(j)
     gg_ref[...] = (tail[...] + dot_t(red[rows:, :], w1_ref[2 * width :, :])).astype(BF16)
     for copy in backs:
         copy.wait_recv()
@@ -293,13 +311,13 @@
     bands, sectors = lax.axis_size("band"), lax.axis_size("sector")
     chips = sectors // 2
     share = w1.shape[0] // (bands * sectors)
-    chunks = width // math.gcd(width, 256)
+    chunks = width // math.gcd(width, LANES)
     wide = width // chunks
     dma = pltpu.SemaphoreType.DMA
     whole = (w1, grid, edge, w2, n1, n2, cot)
     results = pl.pallas_call(
         functools.partial(
-            step_kernel, edge_block=math.gcd(edges, 256), node_block=math.gcd(points, 256)
+            step_kernel, edge_block=math.gcd(edges, 768), node_block=math.gcd(points, 512)
         ),
         out_shape=(
             jax.ShapeDtypeStruct((points, width), BF16),
@@ -317,6 +335,10 @@
             dma((4,)), dma((4,)),
             pltpu.VMEM((rows, width), BF16),
             pltpu.VMEM((rows + points, width), BF16),
+            pltpu.VMEM((width, edges), BF16),
+            pltpu.VMEM((width, points), BF16),
+            pltpu.VMEM((width, rows), BF16),
+            pltpu.VMEM((width, width), BF16),
             pltpu.VMEM((rows + points, edges), BF16),
             pltpu.VMEM((edges, rows + points), BF16),
             pltpu.VMEM((edges, width), F32),

time: 50 us -> 46.9 us (0.938)
  Pallas kernels: 49.2 us -> 46 us
    pallas_call x1, Pallas kernels: 46.7 us -> 43.6 us  [decode_step(): pl.pallas_call(functools.partial(step_kernel, edge_block=math.gcd(edges,...]
where the time goes in v3:
time: 46.9 us; the launch traced here: 46.7 us
  Pallas kernels  46 us (98%)
  between operations  0.64 us (1%)
    pallas_call x1, Pallas kernels, decode_step(): pl.pallas_call(functools.partial(step_kernel, edge_block=math.gcd(edges,...  43.6 us
    pallas_call x1, Pallas kernels, decode_step(): pl.pallas_call(functools.partial(finish_kernel, grad_scale), out_shape=tu...  2.45 us

profile of v3, /device:TPU:0, one launch (start us, length us, event | category | flops | bytes accessed | tf_op | source)
XLA Modules:
  0.0 46.7 jit_solution(17473840648249438723)
XLA Ops:
  0.6 43.6 %shard_map.156 = (bf16[512,512]{1,0:T(8,128)(2,1)}, bf16[512,512]{1,0:T(8,128)(2,1)}, bf16[128,512]{1,0:T(8,128)(2,1)}, bf16[4,48,512]{2,1,0:T(8,128)(2,1)}) custom-call(s32[1536]{0:T(1024)} %src_ref.1, s32[1536]{0:T(1024)} %dst_ref.1, s32[1,128]{1,0:T(1,128)} %bitcast.12, bf16[128,512]{1,0:T(8,128)(2,1)} %own_ref.1, f32[1,512]{1,0:T(1,128)} %bitcast.10, ...), custom_call_target="tpu_custom_call" | custom-call | tf_op jit(solution)/shard_map/pallas_call | solution.py:318
  44.2 2.5 %shard_map.157 = (bf16[512,512]{1,0:T(8,128)(2,1)}, bf16[512,512]{1,0:T(8,128)(2,1)}, bf16[128,512]{1,0:T(8,128)(2,1)}, f32[4,48,512]{2,1,0:T(8,128)}) custom-call(bf16[512,512]{1,0:T(8,128)(2,1)} %get-tuple-element.12.out_in, bf16[512,512]{1,0:T(8,128)(2,1)} %get-tuple-element.13.gg_in, bf16[128,512]{1,0:T(8,128)(2,1)} %get-tuple-element.14.gm_in, ...), custom_call_target="tpu_custom_call" | custom-call | tf_op jit(solution)/shard_map/pallas_call | solution.py:373

commit v4 on v3

--- a/solution.py
+++ b/solution.py
@@ -160,6 +160,8 @@
 
     lax.fori_loop(0, edges // edge_block, prepare, 0)
 
+    loads[3].wait()
+    w2_t[...] = w2_ref[...].T
     for copy in halos:
         copy.wait_recv()
     table[:own, :] = own_ref[...]
@@ -167,8 +169,6 @@
         table[own + g * margin : own + (g + 1) * margin, :] = landed[g]
     proj[:rows, :] = dot(table[...], w1_ref[width : 2 * width, :]).astype(BF16)
     table_t[...] = table[...].T
-    loads[3].wait()
-    w2_t[...] = w2_ref[...].T
 
     def forward(i, carry):
         at = pl.ds(pl.multiple_of(i * edge_block, edge_block), edge_block)
@@ -209,8 +209,7 @@
         at = pl.ds(pl.multiple_of(i * edge_block, edge_block), edge_block)
         dnorm = dot(sel[at, rows:], dagg[...]) * eg_ref[...]
         draw = layer_back(dnorm, xhat[at, :], rstd[at, :1])
-        dhid = dot(draw.astype(BF16), w2_t[...]).astype(BF16).astype(F32)
-        gp[at, :] = (dhid * dsw[at, :]).astype(BF16)
+        msg[at, :] = draw.astype(BF16)
         return carry
 
     lax.fori_loop(0, edges // edge_block, backward, 0)
@@ -241,16 +240,24 @@
     group = math.gcd(chunks, GROUP)
     for c in range(0, chunks, group):
         low, high = c * wide, (c + group) * wide
+
+        def columns(i, carry):
+            at = pl.ds(pl.multiple_of(i * edge_block, edge_block), edge_block)
+            dhid = dot(msg[at, :], w2_t[:, low:high]).astype(BF16).astype(F32)
+            gp[at, low:high] = (dhid * dsw[at, low:high]).astype(BF16)
+            return carry
+
+        lax.fori_loop(0, edges // edge_block, columns, 0)
         grads = gp[:, low:high]
         part = dot(sel_t[...], grads).astype(BF16)
         red[:, low:high] = part
+        for j in range(max(c - group, 0), c):
+            band_stage(j)
         put(c, 0, dot(edge_t[...], grads))
         put(c, width, dot(table_t[...], part[:rows]))
         put(c, 2 * width, dot(grid_t[...], part[rows:]))
         for j in range(c, c + group):
             first.append(send(dw.at[j, :, 1 - core], r0.at[j], s0.at[j], v0.at[j], partner))
-        for j in range(max(c - group, 0), c):
-            band_stage(j)
     grad_table = dot_t(red[:rows, :], w1_ref[width : 2 * width, :])
     for g in range(4):
         gth[g] = grad_table[own + g * margin : own + (g + 1) * margin].astype(BF16)

time: 46.9 us -> 46.6 us (level)
  no operation moved by 1% of the time
where the time goes in v4:
time: 46.6 us; the launch traced here: 46.4 us
  Pallas kernels  45.7 us (98%)
  between operations  0.64 us (1%)
    pallas_call x1, Pallas kernels, decode_step(): pl.pallas_call(functools.partial(step_kernel, edge_block=math.gcd(edges,...  43.3 us
    pallas_call x1, Pallas kernels, decode_step(): pl.pallas_call(functools.partial(finish_kernel, grad_scale), out_shape=tu...  2.45 us

profile of v4, /device:TPU:0, one launch (start us, length us, event | category | flops | bytes accessed | tf_op | source)
XLA Modules:
  0.0 46.4 jit_solution(17516838459386824912)
XLA Ops:
  0.6 43.3 %shard_map.156 = (bf16[512,512]{1,0:T(8,128)(2,1)}, bf16[512,512]{1,0:T(8,128)(2,1)}, bf16[128,512]{1,0:T(8,128)(2,1)}, bf16[4,48,512]{2,1,0:T(8,128)(2,1)}) custom-call(s32[1536]{0:T(1024)} %src_ref.1, s32[1536]{0:T(1024)} %dst_ref.1, s32[1,128]{1,0:T(1,128)} %bitcast.12, bf16[128,512]{1,0:T(8,128)(2,1)} %own_ref.1, f32[1,512]{1,0:T(1,128)} %bitcast.10, ...), custom_call_target="tpu_custom_call" | custom-call | tf_op jit(solution)/shard_map/pallas_call | solution.py:325
  43.9 2.5 %shard_map.157 = (bf16[512,512]{1,0:T(8,128)(2,1)}, bf16[512,512]{1,0:T(8,128)(2,1)}, bf16[128,512]{1,0:T(8,128)(2,1)}, f32[4,48,512]{2,1,0:T(8,128)}) custom-call(bf16[512,512]{1,0:T(8,128)(2,1)} %get-tuple-element.12.out_in, bf16[512,512]{1,0:T(8,128)(2,1)} %get-tuple-element.13.gg_in, bf16[128,512]{1,0:T(8,128)(2,1)} %get-tuple-element.14.gm_in, ...), custom_call_target="tpu_custom_call" | custom-call | tf_op jit(solution)/shard_map/pallas_call | solution.py:380
